TPU v7x, 32 devices: a whole 2x2x4 slice. The times are simulated.
32 devices in a mesh: groups: 2 (over y), cls: 4 (over z), img: 4 (over x, core).
Axes of the slice: x: 2, y: 2, z: 4, core: 2. Of those that a mesh axis runs over, the one named last changes fastest.
Arguments:
- particles: bfloat16 [512, 2, 4608], P(('groups', 'img', 'cls')), parts along dimension 0, may hold values from -30 to 30
- classes: bfloat16 [256, 2, 4608], P(('groups', 'cls')), parts along dimension 0, may hold values from -4 to 4
- ctf: float32 [128, 4608], P('groups'), parts along dimension 0, may hold values from 0.1 to 1
- noise_weight: float32 [9216], P('groups'), parts along dimension 0, may hold values from 0.01 to 0.1
- group_ids: int32 [512], P(('groups', 'img', 'cls')), parts along dimension 0, may hold values from 0 to 63
- shifts: int32 [48, 2], P('groups'), parts along dimension 0, may hold values from -6 to 6
Outputs:
- log_resp: float32 [512, 128], P(('groups', 'img'), 'cls'), parts along dimension 0
- averages: float32 [256, 2, 4608], P(('groups', 'cls'), None, 'img'), parts along dimension 0
There are 2 independent parts, one for each index of `groups`. A program takes and returns all parts, laid end to end along the dimension named above; each array names one. Nothing has to cross between parts.
All inputs are finite; a program needn't handle non-finite values.
Results may differ from a plain program's by a relative error of at most 0.012.
The roundings to bfloat16 on the way count: a program that leaves them out, or rounds other values in their place, can miss the bound.
Values may be sent and summed in bfloat16 or wider, within the bound.
A program may use at most 128 MiB of HBM per device.

v0:
```python
import jax
import jax.numpy as jnp
from jax import lax
from jax.sharding import PartitionSpec as P

BOX = 128
prior_precision = 0.02


def phase_tables(shifts, freq):
    index = jnp.arange(freq)
    along_y = (index // BOX).astype(jnp.float32)
    along_x = (index % BOX - BOX // 2).astype(jnp.float32)
    angle = (
        2.0
        * jnp.pi
        / BOX
        * (
            shifts[:, 0:1].astype(jnp.float32) * along_x[None, :]
            + shifts[:, 1:2].astype(jnp.float32) * along_y[None, :]
        )
    )
    return (jnp.cos(angle), jnp.sin(angle))


def local(particles, classes, ctf, noise_weight, group_ids, shifts):
    part_rows = particles.shape[0]
    freq = particles.shape[2]
    cls_rows = classes.shape[0]
    poses = shifts.shape[0]
    groups = ctf.shape[0]
    total_rows = part_rows * lax.axis_size("cls")
    cos_t, sin_t = phase_tables(shifts, freq)
    real_part = classes[:, 0, :].astype(jnp.float32)
    imag_part = classes[:, 1, :].astype(jnp.float32)
    temp_re = real_part[None] * cos_t[:, None, :] - imag_part[None] * sin_t[:, None, :]
    temp_im = real_part[None] * sin_t[:, None, :] + imag_part[None] * cos_t[:, None, :]
    templates = (
        jnp.stack([temp_re, temp_im], axis=2)
        .astype(jnp.bfloat16)
        .reshape(poses * cls_rows, 2 * freq)
    )
    marks_local = (group_ids[:, None] == jnp.arange(groups)[None, :]).astype(jnp.float32)
    selected = jnp.dot(marks_local, ctf, precision=lax.Precision.HIGHEST)
    weighted = (
        particles.astype(jnp.float32) * (selected * noise_weight[None, :])[:, None, :]
    ).astype(jnp.bfloat16)
    weighted = weighted.reshape(part_rows, 2 * freq)
    marks_low = marks_local.astype(jnp.bfloat16)
    ctf_weight = ctf * ctf * noise_weight[None, :]
    power = jnp.dot(
        ctf_weight,
        (real_part * real_part + imag_part * imag_part).T,
        precision=lax.Precision.HIGHEST,
    )
    gathered, marks_all = (
        lax.all_gather(weighted, "cls", axis=0, tiled=True),
        lax.all_gather(marks_low, "cls", axis=0, tiled=True),
    )
    cross = lax.dot_general(
        gathered, templates, (((1,), (1,)), ((), ())), preferred_element_type=jnp.float32
    )
    penalty = jnp.dot(marks_all.astype(jnp.float32), power, precision=lax.Precision.HIGHEST)
    scores = cross.reshape(gathered.shape[0], poses, cls_rows) - 0.5 * penalty[:, None, :]
    local_peak = jnp.max(scores, axis=(1, 2))
    peak = lax.pmax(local_peak, "cls")
    total = lax.psum(jnp.sum(jnp.exp(scores - peak[:, None, None]), axis=(1, 2)), "cls")
    log_norm = peak + jnp.log(total)
    pose_peak = jnp.max(scores, axis=1)
    log_resp = (
        pose_peak
        + jnp.log(jnp.sum(jnp.exp(scores - pose_peak[:, None, :]), axis=1))
        - log_norm[:, None]
    )
    rho = jnp.exp(scores - log_norm[:, None, None])
    rho_low = rho.astype(jnp.bfloat16).reshape(total_rows, poses * cls_rows)
    pose_total = jnp.sum(rho, axis=1)
    sums = lax.dot_general(
        rho_low, gathered, (((0,), (0,)), ((), ())), preferred_element_type=jnp.float32
    )
    mass_table = jnp.dot(
        pose_total.T, marks_all.astype(jnp.float32), precision=lax.Precision.HIGHEST
    )
    sums = sums.reshape(poses, cls_rows, 2, freq)
    cos_b = cos_t[:, None, :]
    sin_b = sin_t[:, None, :]
    numer_re = jnp.sum(sums[:, :, 0, :] * cos_b + sums[:, :, 1, :] * sin_b, axis=0)
    numer_im = jnp.sum(sums[:, :, 1, :] * cos_b - sums[:, :, 0, :] * sin_b, axis=0)
    numer = jnp.stack([numer_re, numer_im], axis=1)
    denom = jnp.dot(mass_table, ctf_weight, precision=lax.Precision.HIGHEST)
    numer_part, denom_part = (
        lax.psum_scatter(numer, "img", scatter_dimension=2, tiled=True),
        lax.psum_scatter(denom, "img", scatter_dimension=1, tiled=True),
    )
    averages = numer_part / (denom_part[:, None, :] + prior_precision)
    return (log_resp, averages)


def solution(mesh):
    placed = (
        P(("groups", "img", "cls"), None, None),
        P(("groups", "cls"), None, None),
        P("groups", None),
        P("groups"),
        P(("groups", "img", "cls")),
        P("groups", None),
    )
    return jax.shard_map(
        local,
        mesh=mesh,
        in_specs=placed,
        out_specs=(P(("groups", "img"), "cls"), P(("groups", "cls"), None, "img")),
        check_vma=False,
    )
```

profile of v0, /device:TPU:0, one launch (start us, length us, event | category | flops | bytes accessed | tf_op | source)
XLA Modules:
  0.0 220.5 jit_solution(17909339871494409727)
XLA Ops:
  7.2 1.8 convolution_multiply_fusion
  9.0 1.3 multiply_convert_fusion
  10.3 0.7 copy.26
  11.1 2.4 %fusion.34 = (bf16[32,1,4608]{2,1,0:T(2,128)(2,1)S(1)}, bf16[32,1,4608]{2,1,0:T(2,128)(2,1)S(1)}) fusion(bf16[32,2,4608]{2,1,0:T(2,128)(2,1)} %param.7), kind=kLoop, calls=%fused_computation.61 | loop fusion | bytes 1179648 | tf_op jit(solution)/shard_map/slice | solution.py:34
  13.5 0.8 convert_bitcast_fusion.1
  14.3 1.6 fusion.15
  16.0 30.8 %subtract_convert_fusion = (bf16[24,32,1,4608]{3,2,1,0:T(2,128)(2,1)S(1)}, bf16[24,32,1,4608]{3,2,1,0:T(2,128)(2,1)}) fusion(f32[24,4608]{1,0:T(8,128)S(1)} %get-tuple-element.17, f32[32,4608]{1,0:T(8,128)S(1)} %get-tuple-element.22, f32[24,4608]{1,0:T(8,128)S(1)} %get-tuple-element.16, f32[32,4608]{1,0:T(8,128)S(1)} %get-tuple-element.23), kind=kLoop, calls=%fused_computation.6 | loop fusion | flops 28311552 | bytes 16220160 | tf_op jit(solution)/shard_map/convert.2
  46.8 34.8 %pad_maximum_fusion = bf16[24,32,2,4608]{3,2,1,0:T(2,128)(2,1)} fusion(bf16[24,32,1,4608]{3,2,1,0:T(2,128)(2,1)} %get-tuple-element.13, bf16[24,32,1,4608]{3,2,1,0:T(2,128)(2,1)S(1)} %get-tuple-element.12), kind=kLoop, calls=%fused_computation.2 | loop fusion | flops 28311552 | bytes 28311552 | tf_op jit(solution)/shard_map/stack | solution.py:39
  81.6 22.7 %convert_element_type.73 = bf16[24,32,9216]{2,1,0:T(8,128)(2,1)} reshape(bf16[24,32,2,4608]{3,2,1,0:T(2,128)(2,1)} %pad_maximum_fusion) | data formatting | bytes 28311552 | tf_op jit(solution)/shard_map/convert_element_type | solution.py:40
  104.4 14.8 %all_gather.7 = bf16[64,64]{1,0:T(8,128)(2,1)S(1)} all-gather(bf16[16,64]{1,0:T(8,128)(2,1)S(1)} %convert_convert_fusion), channel_id=1, replica_groups=mesh['groups'=2,'cls'=4,'img'=4] {'cls'}, dimensions={0}, use_global_device_ids=true | all-gather | bytes 10240 | tf_op jit(solution)/shard_map/all_gather | solution.py:58
  119.2 1.2 fusion.8
  120.6 7.5 %fusion.35 = (f32[64]{0:T(128)S(1)}, f32[64,24,32]{0,2,1:T(8,128)S(1)}) fusion(f32[64,32]{0,1:T(8,128)S(1)} %convolution_multiply_fusion.1, bf16[24,32,9216]{2,1,0:T(8,128)(2,1)} %convert_element_type.73, bf16[64,9216]{1,0:T(8,128)(2,1)} %all-gather.2.cloned.1.call-done), kind=kOutput, calls=%fused_computation.62 | convolution fusion | flops 906067904 | bytes 15540480 | tf_op jit(solution)/shard_map/dot_general | solution.py:60
  128.1 11.7 %pmax.7 = f32[64]{0:T(128)S(1)} all-reduce(f32[64]{0:T(128)S(1)} %get-tuple-element.20), channel_id=1, replica_groups=mesh['groups'=2,'cls'=4,'img'=4] {'cls'}, use_global_device_ids=true, to_apply=%region_3.4 | all-reduce | flops 64 | bytes 512 | tf_op jit(solution)/shard_map/pmax | solution.py:66
  139.9 8.5 %psum.7 = f32[64]{0:T(128)S(1)} all-reduce(f32[64]{0:T(128)S(1)} %get-tuple-element.10), channel_id=1, replica_groups=mesh['groups'=2,'cls'=4,'img'=4] {'cls'}, use_global_device_ids=true, to_apply=%region_5.6 | all-reduce | flops 64 | bytes 512 | tf_op jit(solution)/shard_map/psum | solution.py:67
  148.6 11.4 %fusion = f32[24,32,2,4608]{3,1,2,0:T(8,128)} fusion(bf16[8,2,8,4608]{3,2,1,0:T(8,128)(2,1)S(1)} %bitcast.71, f32[64,24,32]{0,2,1:T(8,128)S(1)} %get-tuple-element.21, f32[64]{0:T(128)S(1)} %log_add_fusion), kind=kOutput, calls=%fused_computation.9 | convolution fusion | flops 906067968 | bytes 29688064 | tf_op jit(solution)/shard_map/dot_general | solution.py:78
  160.2 1.6 fusion.7
  161.8 10.9 %add_reduce_fusion = (f32[32,4608]{1,0:T(8,128)S(1)}, f32[32,4608]{1,0:T(8,128)S(1)}) fusion(f32[24,32,2,4608]{3,1,2,0:T(8,128)} %fusion, f32[24,4608]{1,0:T(8,128)} %copy-done.2, f32[24,4608]{1,0:T(8,128)S(1)} %get-tuple-element.16), kind=kLoop, calls=%fused_computation.4 | loop fusion | flops 28016640 | bytes 30375936 | tf_op jit(solution)/shard_map/reduce_sum | solution.py:87
  172.8 1.1 pad_maximum_fusion.1
  173.9 0.6 add_subtract_fusion
  174.5 9.2 %reduce-scatter.5.cloned.1.call-done = f32[32,1152]{1,0:T(8,128)} async-done(((f32[32,4608]{1,0:T(8,128)}), f32[32,1152]{1,0:T(8,128)}) %reduce-scatter.5.cloned.1.call-update) | async-done | bytes 147472 | tf_op jit(solution)/shard_map/reduce_scatter | solution.py:93
  183.7 0.9 broadcast_add_fusion
  184.6 27.4 %reduce-scatter.3.cloned.1.call-done = f32[32,2,1152]{2,0,1:T(8,128)} async-done(((f32[32,2,4608]{2,0,1:T(8,128)}), f32[32,2,1152]{2,0,1:T(8,128)}) %reduce-scatter.3.cloned.1.call-update) | async-done | bytes 294928 | tf_op jit(solution)/shard_map/reduce_scatter | solution.py:92
  212.0 1.0 broadcast_divide_fusion
  213.0 0.9 copy.20
  (25 shorter events, 0.9 us)
Async XLA Ops:
  7.2 113.4 %all-gather.2.cloned.1.call-start = ((), (), s32[]{:S(2)}) async-start(), calls=%async_computation.2 | async-start | bytes 1474560 | tf_op jit(solution)/shard_map/all_gather | solution.py:57
  11.0 172.6 %reduce-scatter.5.cloned.1.call-start = ((), (), s32[]{:S(2)}) async-start(), calls=%async_computation.4 | async-start | bytes 737280 | tf_op jit(solution)/shard_map/reduce_scatter | solution.py:93
  16.0 30.8 %copy-start.2 = (f32[24,4608]{1,0:T(8,128)}, f32[24,4608]{1,0:T(8,128)S(1)}, u32[]{:S(2)}) copy-start(f32[24,4608]{1,0:T(8,128)S(1)} %get-tuple-element.17) | copy-start | bytes 1327108
  81.6 22.7 %copy-start.4 = (s32[16]{0:T(128)S(1)}, s32[16]{0:T(128)}, u32[]{:S(2)}) copy-start(s32[16]{0:T(128)} %param.10) | copy-start | bytes 196
  81.6 37.6 %copy-start = (f32[64,4608]{1,0:T(8,128)S(1)}, f32[64,4608]{1,0:T(8,128)}, u32[]{:S(2)}) copy-start(f32[64,4608]{1,0:T(8,128)} %param.8) | copy-start | bytes 3538948
  81.6 37.6 %copy-start.3 = (f32[4608]{0:T(1024)S(1)}, f32[4608]{0:T(1024)}, u32[]{:S(2)}) copy-start(f32[4608]{0:T(1024)} %param.9) | copy-start | bytes 55300
  120.6 28.1 %copy-start.1 = (bf16[64,9216]{1,0:T(8,128)(2,1)S(1)}, bf16[64,9216]{1,0:T(8,128)(2,1)}, u32[]{:S(2)}) copy-start(bf16[64,9216]{1,0:T(8,128)(2,1)} %all-gather.2.cloned.1.call-done) | copy-start | bytes 3538948
  161.8 50.2 %reduce-scatter.3.cloned.1.call-start = ((), (), s32[]{:S(2)}) async-start(), calls=%async_computation.3 | async-start | bytes 1474560 | tf_op jit(solution)/shard_map/reduce_scatter | solution.py:92
Sparse Core Ops, SparseCore 0:
  11.2 33.1 all-gather.1
  161.9 21.7 reduce-scatter.4
  186.3 25.7 reduce-scatter.2
where the time goes:
time: 221 us; the launch traced here: 220 us
  other arithmetic  84.3 us (38%)
  waiting for transfers between devices  36.7 us (17%)
  blocking collectives  35.1 us (16%)
  local copies, waits for them, and re-layouts  26.8 us (12%)
  matrix products  23.7 us (11%)
  between operations  13.9 us (6%)
    another operation x1, other arithmetic, local(): jnp.stack([temp_re, temp_im], axis=2).astype(jnp.bfloat16)  34.8 us
    another operation x1, other arithmetic  30.8 us
    reduce_scatter x1, waiting for transfers between devices, local(): lax.psum_scatter(numer, 'img', scatter_dimension=2, tiled=True)  27.4 us
    convert_element_type x1, local copies, waits for them, and re-layouts, local(): templates = jnp.stack([temp_re, temp_im], axis=2).astype(jnp.bfloat16).re...  22.7 us
    all_gather x1, blocking collectives, local(): lax.all_gather(marks_low, 'cls', axis=0, tiled=True)  14.8 us
    pmax x1, blocking collectives, local(): peak = lax.pmax(local_peak, 'cls')  11.7 us
    dot_general x1, matrix products, local(): lax.dot_general(rho_low, gathered, (((0,), (0,)), ((), ())), preferred_el...  11.4 us
    reduce_sum x1, other arithmetic, local(): jnp.sum(sums[:, :, 0, :] * cos_b + sums[:, :, 1, :] * sin_b, axis=0)  10.9 us
  transfers between devices with their start and end apart: 3, of which 2 were waited for; matrix products, arithmetic and copies ran while one was open for 49% of the time, Pallas kernels for 0%

commit v1 on v0

--- a/solution.py
+++ b/solution.py
@@ -5,6 +5,25 @@
 
 BOX = 128
 prior_precision = 0.02
+
+
+def load_shapes(page, mesh_name):
+    inter = jax.lax.axis_size(mesh_name)
+    base_arr = jax.lax.axis_index(mesh_name)
+    mid_arr, finding = (inter, base_arr)
+    taken_in, tmp = (page, 1)
+    while tmp < mid_arr:
+        shelf = []
+        num = 0
+        while num < mid_arr:
+            shelf.append((num, num ^ tmp))
+            num = num + 1
+        side_arr = jax.lax.ppermute(taken_in, mesh_name, shelf)
+        oldest = jnp.concatenate([taken_in, side_arr], 0)
+        extra = jnp.concatenate([side_arr, taken_in], axis=0)
+        taken_in = jnp.where(finding & tmp == 0, oldest, extra)
+        tmp = 2 * tmp
+    return taken_in
 
 
 def phase_tables(shifts, freq):
@@ -55,7 +74,7 @@
     )
     gathered, marks_all = (
         lax.all_gather(weighted, "cls", axis=0, tiled=True),
-        lax.all_gather(marks_low, "cls", axis=0, tiled=True),
+        load_shapes(marks_low, "cls"),
     )
     cross = lax.dot_general(
         gathered, templates, (((1,), (1,)), ((), ())), preferred_element_type=jnp.float32

time: 221 us -> 210 us (0.950)
  blocking collectives: 35.1 us -> 18.9 us
  starting transfers between devices: 0.12 us -> 5.8 us
    all_gather x1 -> x0, blocking collectives: 14.8 us -> none  [local(): lax.all_gather(marks_low, 'cls', axis=0, tiled=True)]
    ppermute x0 -> x2, starting transfers between devices: none -> 5.68 us  [load_shapes(): side_arr = jax.lax.ppermute(taken_in, mesh_name, shelf)]
    pmax x1, blocking collectives: 11.7 us -> 8.82 us  [local(): peak = lax.pmax(local_peak, 'cls')]
  transfers between devices with their start and end apart: 3 -> 5, of which waited for: 2 -> 2; matrix products, arithmetic and copies ran while one was open for 49% -> 53% of each run, Pallas kernels for 0% -> 0%
where the time goes in v1:
time: 210 us; the launch traced here: 209 us
  other arithmetic  85.1 us (41%)
  waiting for transfers between devices  35.2 us (17%)
  local copies, waits for them, and re-layouts  26.7 us (13%)
  matrix products  23.7 us (11%)
  blocking collectives  18.9 us (9%)
  between operations  13.9 us (7%)
  starting transfers between devices  5.8 us (3%)
    another operation x1, other arithmetic, local(): jnp.stack([temp_re, temp_im], axis=2).astype(jnp.bfloat16)  34.9 us
    another operation x1, other arithmetic  30.8 us
    reduce_scatter x1, waiting for transfers between devices, local(): lax.psum_scatter(numer, 'img', scatter_dimension=2, tiled=True)  27.4 us
    convert_element_type x1, local copies, waits for them, and re-layouts, local(): templates = jnp.stack([temp_re, temp_im], axis=2).astype(jnp.bfloat16).re...  22.6 us
    dot_general x1, matrix products, local(): lax.dot_general(rho_low, gathered, (((0,), (0,)), ((), ())), preferred_el...  11.4 us
    reduce_sum x1, other arithmetic, local(): jnp.sum(sums[:, :, 0, :] * cos_b + sums[:, :, 1, :] * sin_b, axis=0)  10.9 us
    psum x1, blocking collectives, local(): lax.psum(jnp.sum(jnp.exp(scores - peak[:, None, None]), axis=(1, 2)), 'cls')  10.1 us
    pmax x1, blocking collectives, local(): peak = lax.pmax(local_peak, 'cls')  8.82 us
  transfers between devices with their start and end apart: 5, of which 2 were waited for; matrix products, arithmetic and copies ran while one was open for 53% of the time, Pallas kernels for 0%

profile of v1, /device:TPU:0, one launch (start us, length us, event | category | flops | bytes accessed | tf_op | source)
XLA Modules:
  0.0 209.2 jit_solution(1938288387920021132)
XLA Ops:
  7.9 3.0 %collective-permute-start = (bf16[16,64]{1,0:T(8,128)(2,1)S(1)}, bf16[16,64]{1,0:T(8,128)(2,1)S(1)}, u32[]{:S(2)}, u32[]{:S(2)}) collective-permute-start(bf16[16,64]{1,0:T(8,128)(2,1)S(1)} %convert_convert_fusion), channel_id=1, source_target_pairs={{0,4},{4,0},{8,12},{12,8},{1,5},{5,1},{9,13},{13,9},{2,6},{6,2},{1... | collective-permute-start | bytes 6152 | tf_op jit(solution)/shard_map/ppermute | solution.py:21
  11.0 1.8 convolution_multiply_fusion
  12.7 1.3 multiply_convert_fusion
  14.0 0.7 copy.26
  14.9 2.4 %fusion.37 = (bf16[32,1,4608]{2,1,0:T(2,128)(2,1)S(1)}, bf16[32,1,4608]{2,1,0:T(2,128)(2,1)S(1)}) fusion(bf16[32,2,4608]{2,1,0:T(2,128)(2,1)} %param.7), kind=kLoop, calls=%fused_computation.66 | loop fusion | bytes 1179648 | tf_op jit(solution)/shard_map/slice | solution.py:53
  17.2 0.8 convert_bitcast_fusion.1
  18.1 1.6 fusion.15
  19.7 30.8 %subtract_convert_fusion = (bf16[24,32,1,4608]{3,2,1,0:T(2,128)(2,1)S(1)}, bf16[24,32,1,4608]{3,2,1,0:T(2,128)(2,1)}) fusion(f32[24,4608]{1,0:T(8,128)S(1)} %get-tuple-element.17, f32[32,4608]{1,0:T(8,128)S(1)} %get-tuple-element.22, f32[24,4608]{1,0:T(8,128)S(1)} %get-tuple-element.16, f32[32,4608]{1,0:T(8,128)S(1)} %get-tuple-element.23), kind=kLoop, calls=%fused_computation.6 | loop fusion | flops 28311552 | bytes 16220160 | tf_op jit(solution)/shard_map/convert.2
  50.6 34.9 %pad_maximum_fusion = bf16[24,32,2,4608]{3,2,1,0:T(2,128)(2,1)} fusion(bf16[24,32,1,4608]{3,2,1,0:T(2,128)(2,1)} %get-tuple-element.13, bf16[24,32,1,4608]{3,2,1,0:T(2,128)(2,1)S(1)} %get-tuple-element.12), kind=kLoop, calls=%fused_computation.2 | loop fusion | flops 28311552 | bytes 28311552 | tf_op jit(solution)/shard_map/stack | solution.py:58
  85.5 2.7 %collective-permute-start.1 = (bf16[32,64]{1,0:T(8,128)(2,1)S(1)}, bf16[32,64]{1,0:T(8,128)(2,1)S(1)}, u32[]{:S(2)}, u32[]{:S(2)}) collective-permute-start(bf16[32,64]{1,0:T(8,128)(2,1)S(1)} %maximum_select_fusion.1), channel_id=1, source_target_pairs={{0,8},{4,12},{8,0},{12,4},{1,9},{5,13},{9,1},{13,5},{2,10},{6,14},... | collective-permute-start | bytes 12296 | tf_op jit(solution)/shard_map/ppermute | solution.py:21
  88.2 1.2 fusion.8
  89.3 22.6 %convert_element_type.73 = bf16[24,32,9216]{2,1,0:T(8,128)(2,1)} reshape(bf16[24,32,2,4608]{3,2,1,0:T(2,128)(2,1)} %pad_maximum_fusion) | data formatting | bytes 28311552 | tf_op jit(solution)/shard_map/convert_element_type | solution.py:59
  112.1 7.5 %fusion.38 = (f32[64]{0:T(128)S(1)}, f32[64,24,32]{0,2,1:T(8,128)S(1)}) fusion(f32[64,32]{0,1:T(8,128)S(1)} %convolution_multiply_fusion.1, bf16[24,32,9216]{2,1,0:T(8,128)(2,1)} %convert_element_type.73, bf16[64,9216]{1,0:T(8,128)(2,1)} %all-gather.2.cloned.1.call-done), kind=kOutput, calls=%fused_computation.67 | convolution fusion | flops 906067904 | bytes 15540480 | tf_op jit(solution)/shard_map/dot_general | solution.py:79
  119.6 8.8 %pmax.7 = f32[64]{0:T(128)S(1)} all-reduce(f32[64]{0:T(128)S(1)} %get-tuple-element.20), channel_id=1, replica_groups=mesh['groups'=2,'cls'=4,'img'=4] {'cls'}, use_global_device_ids=true, to_apply=%region_3.4 | all-reduce | flops 64 | bytes 512 | tf_op jit(solution)/shard_map/pmax | solution.py:85
  128.6 10.1 %psum.7 = f32[64]{0:T(128)S(1)} all-reduce(f32[64]{0:T(128)S(1)} %get-tuple-element.10), channel_id=1, replica_groups=mesh['groups'=2,'cls'=4,'img'=4] {'cls'}, use_global_device_ids=true, to_apply=%region_5.6 | all-reduce | flops 64 | bytes 512 | tf_op jit(solution)/shard_map/psum | solution.py:86
  138.8 11.4 %fusion = f32[24,32,2,4608]{3,1,2,0:T(8,128)} fusion(bf16[8,2,8,4608]{3,2,1,0:T(8,128)(2,1)S(1)} %bitcast.69, f32[64,24,32]{0,2,1:T(8,128)S(1)} %get-tuple-element.21, f32[64]{0:T(128)S(1)} %log_add_fusion), kind=kOutput, calls=%fused_computation.9 | convolution fusion | flops 906067968 | bytes 29688064 | tf_op jit(solution)/shard_map/dot_general | solution.py:97
  150.4 1.6 fusion.7
  152.0 10.9 %add_reduce_fusion = (f32[32,4608]{1,0:T(8,128)S(1)}, f32[32,4608]{1,0:T(8,128)S(1)}) fusion(f32[24,32,2,4608]{3,1,2,0:T(8,128)} %fusion, f32[24,4608]{1,0:T(8,128)} %copy-done.2, f32[24,4608]{1,0:T(8,128)S(1)} %get-tuple-element.16), kind=kLoop, calls=%fused_computation.4 | loop fusion | flops 28016640 | bytes 30375936 | tf_op jit(solution)/shard_map/reduce_sum | solution.py:106
  163.0 1.1 pad_maximum_fusion.1
  164.7 7.7 %reduce-scatter.5.cloned.1.call-done = f32[32,1152]{1,0:T(8,128)} async-done(((f32[32,4608]{1,0:T(8,128)}), f32[32,1152]{1,0:T(8,128)}) %reduce-scatter.5.cloned.1.call-update) | async-done | bytes 147472 | tf_op jit(solution)/shard_map/reduce_scatter | solution.py:112
  172.4 0.9 broadcast_add_fusion
  173.3 27.4 %reduce-scatter.3.cloned.1.call-done = f32[32,2,1152]{2,0,1:T(8,128)} async-done(((f32[32,2,4608]{2,0,1:T(8,128)}), f32[32,2,1152]{2,0,1:T(8,128)}) %reduce-scatter.3.cloned.1.call-update) | async-done | bytes 294928 | tf_op jit(solution)/shard_map/reduce_scatter | solution.py:111
  200.7 1.0 broadcast_divide_fusion
  201.7 0.9 copy.20
  (27 shorter events, 2.2 us)
Async XLA Ops:
  7.2 104.9 %all-gather.2.cloned.1.call-start = ((), (), s32[]{:S(2)}) async-start(), calls=%async_computation.2 | async-start | bytes 1474560 | tf_op jit(solution)/shard_map/all_gather | solution.py:76
  7.9 77.5 %collective-permute-start = (bf16[16,64]{1,0:T(8,128)(2,1)S(1)}, bf16[16,64]{1,0:T(8,128)(2,1)S(1)}, u32[]{:S(2)}, u32[]{:S(2)}) collective-permute-start(bf16[16,64]{1,0:T(8,128)(2,1)S(1)} %convert_convert_fusion), channel_id=1, source_target_pairs={{0,4},{4,0},{8,12},{12,8},{1,5},{5,1},{9,13},{13,9},{2,6},{6,2},{1... | collective-permute-start | bytes 6152 | tf_op jit(solution)/shard_map/ppermute | solution.py:21
  14.8 157.6 %reduce-scatter.5.cloned.1.call-start = ((), (), s32[]{:S(2)}) async-start(), calls=%async_computation.4 | async-start | bytes 737280 | tf_op jit(solution)/shard_map/reduce_scatter | solution.py:112
  19.7 30.8 %copy-start.2 = (f32[24,4608]{1,0:T(8,128)}, f32[24,4608]{1,0:T(8,128)S(1)}, u32[]{:S(2)}) copy-start(f32[24,4608]{1,0:T(8,128)S(1)} %get-tuple-element.17) | copy-start | bytes 1327108
  50.6 37.6 %copy-start = (f32[64,4608]{1,0:T(8,128)S(1)}, f32[64,4608]{1,0:T(8,128)}, u32[]{:S(2)}) copy-start(f32[64,4608]{1,0:T(8,128)} %param.8) | copy-start | bytes 3538948
  50.6 37.6 %copy-start.3 = (f32[4608]{0:T(1024)S(1)}, f32[4608]{0:T(1024)}, u32[]{:S(2)}) copy-start(f32[4608]{0:T(1024)} %param.9) | copy-start | bytes 55300
  85.5 26.4 %collective-permute-start.1 = (bf16[32,64]{1,0:T(8,128)(2,1)S(1)}, bf16[32,64]{1,0:T(8,128)(2,1)S(1)}, u32[]{:S(2)}, u32[]{:S(2)}) collective-permute-start(bf16[32,64]{1,0:T(8,128)(2,1)S(1)} %maximum_select_fusion.1), channel_id=1, source_target_pairs={{0,8},{4,12},{8,0},{12,4},{1,9},{5,13},{9,1},{13,5},{2,10},{6,14},... | collective-permute-start | bytes 12296 | tf_op jit(solution)/shard_map/ppermute | solution.py:21
  112.1 26.7 %copy-start.1 = (bf16[64,9216]{1,0:T(8,128)(2,1)S(1)}, bf16[64,9216]{1,0:T(8,128)(2,1)}, u32[]{:S(2)}) copy-start(bf16[64,9216]{1,0:T(8,128)(2,1)} %all-gather.2.cloned.1.call-done) | copy-start | bytes 3538948
  152.0 48.8 %reduce-scatter.3.cloned.1.call-start = ((), (), s32[]{:S(2)}) async-start(), calls=%async_computation.3 | async-start | bytes 1474560 | tf_op jit(solution)/shard_map/reduce_scatter | solution.py:111
Sparse Core Ops, SparseCore 0:
  14.9 30.6 all-gather.1
  152.1 20.2 reduce-scatter.4
  175.0 25.7 reduce-scatter.2
